TPU v7x, 32 devices: a whole 2x2x4 slice. The times are simulated.
32 devices in a mesh: wide: 8 (over y, x, core), narrow: 4 (over z).
Axes of the slice: x: 2, y: 2, z: 4, core: 2. Of those that a mesh axis runs over, the one named last changes fastest.
Arguments:
- hidden_in: bfloat16 [16, 1024, 768], P('wide', 'narrow'), may hold values from -6 to 6
- positions: int32 [16, 1024], P('wide', 'narrow'), may hold values from 0 to 1023, as said below
- time_index: int32 [16], P('wide'), may hold values from 0 to 1023
- cond_table: bfloat16 [1024, 128], replicated, may hold values from -5 to 5
- ada_weight: bfloat16 [128, 4608], replicated, may hold values from -0.5 to 0.5
- norm1_gain: bfloat16 [768], replicated, may hold values from 0.099609375 to 1.8984375
- qkv_weight: bfloat16 [768, 2304], replicated, may hold values from -0.21875 to 0.21875
- out_weight: bfloat16 [768, 768], replicated, may hold values from -0.875 to 0.875
- norm2_gain: bfloat16 [768], replicated, may hold values from 0.099609375 to 1.8984375
- up_weight: bfloat16 [768, 3072], replicated, may hold values from -0.21875 to 0.21875
- down_weight: bfloat16 [3072, 768], replicated, may hold values from -0.21875 to 0.21875
- cotangent: bfloat16 [16, 1024, 768], P('wide', 'narrow'), may hold values from -6 to 6
Outputs:
- hidden_out: bfloat16 [16, 1024, 768], P('wide', 'narrow')
- hidden_grad: bfloat16 [16, 1024, 768], P('wide', 'narrow')
- cond_table_grad: float32 [1024, 128], P('wide', 'narrow')
- ada_weight_grad: float32 [128, 4608], P('narrow', 'wide')
- norm1_gain_grad: float32 [768], P('wide')
- qkv_weight_grad: float32 [768, 2304], P('wide', 'narrow')
- out_weight_grad: float32 [768, 768], P('wide', 'narrow')
- norm2_gain_grad: float32 [768], P('wide')
- up_weight_grad: float32 [768, 3072], P('wide', 'narrow')
- down_weight_grad: float32 [3072, 768], P('wide', 'narrow')
Inputs may be any that keep to these rules, and one draw needn't show every extreme that they name: positions count up by one from the start of each packed document, every row starts a document at its first token, and one row is a single document.
All inputs are finite; a program needn't handle non-finite values.
Results may differ from a plain program's by a relative error of at most 0.015.
The roundings to bfloat16 on the way count: a program that leaves them out, or rounds other values in their place, can miss the bound.
Values may be sent and summed in bfloat16 or wider, within the bound.
No kernel may reach another device: no remote copies, remote signals or barrier semaphores. Data moves between devices by JAX's collectives and lax.ppermute only.
A program may use at most 192 MiB of HBM per device.

v0:
```python
import jax
import jax.numpy as jnp
from jax import lax
from jax.sharding import PartitionSpec as P

HEAD_DIM = 64
HIGHEST = lax.Precision.HIGHEST
norm_eps = 1e-05


def norm_mod(hidden, gain, shift, scale):
    center = hidden - jnp.mean(hidden, axis=-1, keepdims=True)
    variance = jnp.mean(center * center, axis=-1, keepdims=True)
    return center * lax.rsqrt(variance + norm_eps) * gain * (1.0 + scale) + shift


def rotary(values, positions):
    half_dim = values.shape[-1] // 2
    frequency = 10000.0 ** (-jnp.arange(half_dim, dtype=jnp.float32) / half_dim)
    angles = positions.astype(jnp.float32)[..., None, None] * frequency
    cosine = jnp.cos(angles)
    sine = jnp.sin(angles)
    first_half = values[..., :half_dim]
    second_half = values[..., half_dim:]
    return jnp.concatenate(
        [first_half * cosine - second_half * sine, second_half * cosine + first_half * sine],
        axis=-1,
    )


def gelu_tanh(values):
    return jax.nn.gelu(values, approximate=True)


def tdot(left, right):
    return lax.dot_general(
        left, right, (((0,), (0,)), ((), ())), preferred_element_type=jnp.float32
    )


def ndot(left, right):
    return lax.dot_general(
        left, right, (((1,), (1,)), ((), ())), preferred_element_type=jnp.float32
    )


def attend(row_item):
    queries, key_rows, value_rows = row_item
    length = queries.shape[0]
    local_heads = queries.shape[1] // HEAD_DIM
    queries = queries.reshape(length, local_heads, HEAD_DIM)
    key_rows = key_rows.reshape(length, local_heads, HEAD_DIM)
    value_rows = value_rows.reshape(length, local_heads, HEAD_DIM)
    scores = jnp.einsum(
        "qhd,khd->hqk", queries, key_rows, preferred_element_type=jnp.float32
    ) * HEAD_DIM ** (-0.5)
    row_max = jnp.max(scores, axis=-1, keepdims=True)
    expo = jnp.exp(scores - row_max)
    row_total = jnp.sum(expo, axis=-1, keepdims=True)
    probs = expo / row_total
    log_total = row_max + jnp.log(row_total)
    result = jnp.einsum(
        "hqk,khd->qhd", probs.astype(jnp.bfloat16), value_rows, preferred_element_type=jnp.float32
    )
    return (result.astype(jnp.bfloat16).reshape(length, local_heads * HEAD_DIM), log_total)


def attend_back(row_item):
    queries, key_rows, value_rows, d_result, log_total = row_item
    length = queries.shape[0]
    local_heads = queries.shape[1] // HEAD_DIM
    queries = queries.reshape(length, local_heads, HEAD_DIM)
    key_rows = key_rows.reshape(length, local_heads, HEAD_DIM)
    value_rows = value_rows.reshape(length, local_heads, HEAD_DIM)
    d_result = d_result.reshape(length, local_heads, HEAD_DIM)
    score_scale = HEAD_DIM ** (-0.5)
    scores = (
        jnp.einsum("qhd,khd->hqk", queries, key_rows, preferred_element_type=jnp.float32)
        * score_scale
    )
    probs = jnp.exp(scores - log_total)
    d_values = jnp.einsum(
        "hqk,qhd->khd", probs.astype(jnp.bfloat16), d_result, preferred_element_type=jnp.float32
    )
    d_probs = jnp.einsum("qhd,khd->hqk", d_result, value_rows, preferred_element_type=jnp.float32)
    d_scores = probs * (d_probs - jnp.sum(probs * d_probs, axis=-1, keepdims=True))
    d_low = d_scores.astype(jnp.bfloat16)
    d_queries = (
        jnp.einsum("hqk,khd->qhd", d_low, key_rows, preferred_element_type=jnp.float32)
        * score_scale
    )
    d_keys = (
        jnp.einsum("hqk,qhd->khd", d_low, queries, preferred_element_type=jnp.float32) * score_scale
    )
    width_local = local_heads * HEAD_DIM
    return (
        d_queries.astype(jnp.bfloat16).reshape(length, width_local),
        d_keys.astype(jnp.bfloat16).reshape(length, width_local),
        d_values.astype(jnp.bfloat16).reshape(length, width_local),
    )


def blocks_rows_wide(grad, wide_count, narrow_count):
    rows, cols = grad.shape
    split = grad.reshape(wide_count, rows // wide_count, narrow_count, cols // narrow_count)
    return split.transpose(0, 2, 1, 3).reshape(wide_count, narrow_count, -1)


def blocks_rows_narrow(grad, wide_count, narrow_count):
    rows, cols = grad.shape
    split = grad.reshape(narrow_count, rows // narrow_count, wide_count, cols // wide_count)
    return split.transpose(2, 0, 1, 3).reshape(wide_count, narrow_count, -1)


def blocks_gain(grad, wide_count, narrow_count):
    split = grad.reshape(wide_count, 1, grad.shape[0] // wide_count)
    return jnp.broadcast_to(split, (wide_count, narrow_count, grad.shape[0] // wide_count))


def on_device(
    hidden_in,
    positions,
    time_index,
    cond_table,
    ada_weight,
    norm1_gain,
    qkv_weight,
    out_weight,
    norm2_gain,
    up_weight,
    down_weight,
    cotangent,
):
    row_count, part_len, model_width = hidden_in.shape
    tokens = row_count * part_len
    heads_all = model_width // HEAD_DIM
    times = cond_table.shape[0]
    onehot = (time_index[:, None] == jnp.arange(times, dtype=jnp.int32)[None, :]).astype(
        jnp.float32
    )
    embedded = jnp.dot(
        onehot,
        cond_table.astype(jnp.float32),
        precision=HIGHEST,
        preferred_element_type=jnp.float32,
    )
    condition_low = jax.nn.silu(embedded).astype(jnp.bfloat16)
    modulation = jnp.dot(condition_low, ada_weight, preferred_element_type=jnp.float32)
    pieces = [
        modulation[:, None, index * model_width : (index + 1) * model_width] for index in range(6)
    ]
    shift_one, scale_one, gate_one, shift_two, scale_two, gate_two = pieces
    hidden_full = hidden_in.astype(jnp.float32)
    gain_one = norm1_gain.astype(jnp.float32)
    gain_two = norm2_gain.astype(jnp.float32)
    norm_one = (
        norm_mod(hidden_full, gain_one, shift_one, scale_one)
        .astype(jnp.bfloat16)
        .reshape(tokens, model_width)
    )
    qkv = jnp.dot(norm_one, qkv_weight, preferred_element_type=jnp.float32).reshape(
        row_count, part_len, 3, heads_all, HEAD_DIM
    )
    query_pre = qkv[:, :, 0]
    key_pre = qkv[:, :, 1]
    query_low = (
        rotary(query_pre, positions).astype(jnp.bfloat16).reshape(row_count, part_len, model_width)
    )
    key_low = (
        rotary(key_pre, positions).astype(jnp.bfloat16).reshape(row_count, part_len, model_width)
    )
    value_low = qkv[:, :, 2].astype(jnp.bfloat16).reshape(row_count, part_len, model_width)
    query_heads, key_heads, value_heads = (
        lax.all_to_all(query_low, "narrow", split_axis=2, concat_axis=1, tiled=True),
        lax.all_to_all(key_low, "narrow", split_axis=2, concat_axis=1, tiled=True),
        lax.all_to_all(value_low, "narrow", split_axis=2, concat_axis=1, tiled=True),
    )
    attended_heads, log_totals = lax.map(attend, (query_heads, key_heads, value_heads))
    attended = lax.all_to_all(
        attended_heads, "narrow", split_axis=1, concat_axis=2, tiled=True
    ).reshape(tokens, model_width)
    projected = jnp.dot(attended, out_weight, preferred_element_type=jnp.float32).reshape(
        row_count, part_len, model_width
    )
    middle = hidden_full + gate_one * projected
    norm_two = (
        norm_mod(middle, gain_two, shift_two, scale_two)
        .astype(jnp.bfloat16)
        .reshape(tokens, model_width)
    )
    up_part = jnp.dot(norm_two, up_weight, preferred_element_type=jnp.float32)
    activated = gelu_tanh(up_part).astype(jnp.bfloat16)
    down_part = jnp.dot(activated, down_weight, preferred_element_type=jnp.float32).reshape(
        row_count, part_len, model_width
    )
    hidden_out = (middle + gate_two * down_part).astype(jnp.bfloat16)
    d_out = cotangent.astype(jnp.float32)
    d_gate_two = jnp.sum(d_out * down_part, axis=1)
    d_down = (d_out * gate_two).astype(jnp.bfloat16).reshape(tokens, model_width)
    grad_down = tdot(activated, d_down)
    d_activated = ndot(d_down, down_weight)
    unused_gelu, gelu_back = jax.vjp(gelu_tanh, up_part)
    d_up = gelu_back(d_activated)[0].astype(jnp.bfloat16)
    grad_up = tdot(norm_two, d_up)
    d_norm_two = ndot(d_up, up_weight).reshape(row_count, part_len, model_width)
    unused_two, norm_two_back = jax.vjp(norm_mod, middle, gain_two, shift_two, scale_two)
    d_middle_norm, grad_gain_two, d_shift_two, d_scale_two = norm_two_back(d_norm_two)
    d_middle = d_out + d_middle_norm
    d_gate_one = jnp.sum(d_middle * projected, axis=1)
    d_projected = (d_middle * gate_one).astype(jnp.bfloat16).reshape(tokens, model_width)
    grad_out = tdot(attended, d_projected)
    d_attended = (
        ndot(d_projected, out_weight).astype(jnp.bfloat16).reshape(row_count, part_len, model_width)
    )
    d_attended_heads = lax.all_to_all(d_attended, "narrow", split_axis=2, concat_axis=1, tiled=True)
    d_query_heads, d_key_heads, d_value_heads = lax.map(
        attend_back, (query_heads, key_heads, value_heads, d_attended_heads, log_totals)
    )
    d_query, d_key, d_value = (
        lax.all_to_all(d_query_heads, "narrow", split_axis=1, concat_axis=2, tiled=True),
        lax.all_to_all(d_key_heads, "narrow", split_axis=1, concat_axis=2, tiled=True),
        lax.all_to_all(d_value_heads, "narrow", split_axis=1, concat_axis=2, tiled=True),
    )

    def rotate_both(query_part, key_part):
        return (rotary(query_part, positions), rotary(key_part, positions))

    unused_rot, rotate_back = jax.vjp(rotate_both, query_pre, key_pre)
    head_shape = (row_count, part_len, heads_all, HEAD_DIM)
    d_query_pre, d_key_pre = rotate_back(
        (
            d_query.astype(jnp.float32).reshape(head_shape),
            d_key.astype(jnp.float32).reshape(head_shape),
        )
    )
    d_qkv = jnp.stack(
        [d_query_pre, d_key_pre, d_value.astype(jnp.float32).reshape(head_shape)], axis=2
    )
    d_qkv = d_qkv.astype(jnp.bfloat16).reshape(tokens, 3 * model_width)
    grad_qkv = tdot(norm_one, d_qkv)
    d_norm_one = ndot(d_qkv, qkv_weight).reshape(row_count, part_len, model_width)
    unused_one, norm_one_back = jax.vjp(norm_mod, hidden_full, gain_one, shift_one, scale_one)
    d_hidden_norm, grad_gain_one, d_shift_one, d_scale_one = norm_one_back(d_norm_one)
    hidden_grad = (d_middle + d_hidden_norm).astype(jnp.bfloat16)
    d_modulation = jnp.concatenate(
        [
            d_shift_one.reshape(row_count, model_width),
            d_scale_one.reshape(row_count, model_width),
            d_gate_one,
            d_shift_two.reshape(row_count, model_width),
            d_scale_two.reshape(row_count, model_width),
            d_gate_two,
        ],
        axis=1,
    )
    grad_ada = lax.dot_general(
        condition_low.astype(jnp.float32),
        d_modulation,
        (((0,), (0,)), ((), ())),
        precision=HIGHEST,
        preferred_element_type=jnp.float32,
    )
    d_condition = lax.dot_general(
        d_modulation,
        ada_weight.astype(jnp.float32),
        (((1,), (1,)), ((), ())),
        precision=HIGHEST,
        preferred_element_type=jnp.float32,
    )
    unused_silu, silu_back = jax.vjp(jax.nn.silu, embedded)
    d_embedded = silu_back(d_condition)[0]
    grad_table = lax.dot_general(
        onehot,
        d_embedded,
        (((0,), (0,)), ((), ())),
        precision=HIGHEST,
        preferred_element_type=jnp.float32,
    )
    wide_count = lax.axis_size("wide")
    narrow_count = lax.axis_size("narrow")
    weight_grads = [
        grad_table,
        grad_ada,
        grad_gain_one,
        grad_qkv,
        grad_out,
        grad_gain_two,
        grad_up,
        grad_down,
    ]
    kinds = ["wide", "narrow", "gain", "wide", "wide", "gain", "wide", "wide"]
    block_list = []
    local_shapes = []
    for item, kind in zip(weight_grads, kinds):
        if kind == "wide":
            block_list.append(blocks_rows_wide(item, wide_count, narrow_count))
            local_shapes.append((item.shape[0] // wide_count, item.shape[1] // narrow_count))
        elif kind == "narrow":
            block_list.append(blocks_rows_narrow(item, wide_count, narrow_count))
            local_shapes.append((item.shape[0] // narrow_count, item.shape[1] // wide_count))
        else:
            block_list.append(blocks_gain(item, wide_count, narrow_count))
            local_shapes.append((item.shape[0] // wide_count,))
    stacked = jnp.concatenate(block_list, axis=2)
    joined = stacked.reshape(wide_count * narrow_count, stacked.shape[2])
    summed = lax.psum_scatter(joined, ("wide", "narrow"), scatter_dimension=0, tiled=True).reshape(
        -1
    )
    results = []
    offset = 0
    for shape in local_shapes:
        count = 1
        for extent in shape:
            count = count * extent
        results.append(summed[offset : offset + count].reshape(shape))
        offset = offset + count
    return (
        hidden_out,
        hidden_grad,
        results[0],
        results[1],
        results[2],
        results[3],
        results[4],
        results[5],
        results[6],
        results[7],
    )


def solution(mesh):
    in_specs = (
        P("wide", "narrow", None),
        P("wide", "narrow"),
        P("wide"),
        P(),
        P(),
        P(),
        P(),
        P(),
        P(),
        P(),
        P(),
        P("wide", "narrow", None),
    )
    out_specs = (
        P("wide", "narrow", None),
        P("wide", "narrow", None),
        P("wide", "narrow"),
        P("narrow", "wide"),
        P("wide"),
        P("wide", "narrow"),
        P("wide", "narrow"),
        P("wide"),
        P("wide", "narrow"),
        P("wide", "narrow"),
    )
    return jax.shard_map(
        on_device, mesh=mesh, in_specs=in_specs, out_specs=out_specs, check_vma=False
    )
```

profile of v0, /device:TPU:0, one launch (start us, length us, event | category | flops | bytes accessed | tf_op | source)
XLA Modules:
  0.0 1036.6 jit_solution(18273378319542742261)
XLA Ops:
  24.7 6.3 all-to-all-start
  36.9 14.2 %all-to-all-done = bf16[2,256,768]{1,0,2:T(2,128)(2,1)S(1)} async-done(((bf16[2,256,768]{1,0,2:T(2,128)(2,1)}), bf16[2,256,768]{1,0,2:T(2,128)(2,1)S(1)}, u32[]{:S(2)}, u32[]{:S(2)}) %all-to-all-start) | async-done | bytes 786464 | tf_op jit(solution)/shard_map/all_to_all | solution.py:176
  57.5 16.7 %all-to-all-done.1 = bf16[2,256,768]{1,0,2:T(2,128)(2,1)S(1)} async-done(((bf16[2,256,768]{1,0,2:T(2,128)(2,1)}), bf16[2,256,768]{1,0,2:T(2,128)(2,1)S(1)}, u32[]{:S(2)}, u32[]{:S(2)}) %all-to-all-start.1) | async-done | bytes 786464 | tf_op jit(solution)/shard_map/all_to_all | solution.py:174
  85.6 13.0 %all-to-all-done.2 = bf16[2,256,768]{1,0,2:T(2,128)(2,1)} async-done(((bf16[2,256,768]{1,0,2:T(2,128)(2,1)}), bf16[2,256,768]{1,0,2:T(2,128)(2,1)}, u32[]{:S(2)}, u32[]{:S(2)}) %all-to-all-start.2) | async-done | bytes 786464 | tf_op jit(solution)/shard_map/all_to_all | solution.py:175
  104.7 17.3 %while.26 = (s32[]{:T(128)}, bf16[2,1024,192]{1,2,0:T(8,128)(2,1)}, f32[2,3,1024,1]{2,1,3,0:T(4,128)}, bf16[2,1024,192]{1,2,0:T(8,128)(2,1)S(1)}, bf16[2,1024,19...) while((s32[]{:T(128)}, bf16[2,1024,192]{1,2,0:T(8,128)(2,1)}, ...), condition=%wide.region_5.6_spmd, body=%wide.region_2.5_spmd.sunk | while | flops 833811456 | bytes 48861340 | solution.py:178
  130.1 7.9 fusion.85
  137.9 17.4 %all-to-all-done.3 = bf16[2,1024,192]{2,0,1:T(2,128)(2,1)} async-done(((bf16[2,1024,192]{2,0,1:T(2,128)(2,1)}), bf16[2,1024,192]{2,0,1:T(2,128)(2,1)}, u32[]{:S(2)}, u32[]{:S(2)}) %all-to-all-start.3) | async-done | bytes 786464 | tf_op jit(solution)/shard_map/all_to_all | solution.py:179
  164.0 12.8 %fusion.27 = (bf16[3072,512]{0,1:T(8,128)(2,1)}, bf16[3072,512]{0,1:T(8,128)(2,1)}, f32[512,3072]{1,0:T(8,128)}) fusion(f32[512,3072]{1,0:T(8,128)S(1)} %copy-done.64, bf16[512,768]{1,0:T(8,128)(2,1)S(1)} %bitcast.357, bf16[768,3072]{1,0:T(8,128)(2,1)} %param.25), kind=kOutput, calls=%fused_computation.51 | convolution fusion | flops 2450522112 | bytes 24379392 | tf_op jit(solution)/shard_map/dot_general | solution.py:191
  176.8 8.4 fusion.34
  185.3 6.3 fusion.33
  202.4 22.1 %all_to_all.114 = bf16[2,256,768]{1,0,2:T(2,128)(2,1)S(1)} all-to-all(bf16[2,256,768]{1,0,2:T(2,128)(2,1)S(1)} %copy.123), channel_id=1, replica_groups=mesh['wide'=8,'narrow'=4] {'narrow'}, dimensions={2} | all-to-all | bytes 1572864 | tf_op jit(solution)/shard_map/all_to_all | solution.py:215
  228.5 46.5 %while.27 = (s32[]{:T(128)}, bf16[2,1024,192]{1,2,0:T(8,128)(2,1)}, bf16[2,1024,192]{1,2,0:T(8,128)(2,1)}, bf16[2,1024,192]{1,2,0:T(8,128)(2,1)}, bf16[2,1024,19...) while((s32[]{:T(128)}, bf16[2,1024,192]{1,2,0:T(8,128)(2,1)}, ...), condition=%wide.region_12.13_spmd, body=%wide.region_10.12_spmd.sunk | while | flops 2051994624 | bytes 144789888 | solution.py:216
  284.3 22.7 %all-to-all-done.7 = bf16[2,1024,192]{2,0,1:T(2,128)(2,1)S(1)} async-done(((bf16[2,1024,192]{2,0,1:T(2,128)(2,1)}), bf16[2,1024,192]{2,0,1:T(2,128)(2,1)S(1)}, u32[]{:S(2)}, u32[]{:S(2)}) %all-to-all-start.7) | async-done | bytes 786464 | tf_op jit(solution)/shard_map/all_to_all | solution.py:222
  322.2 13.7 %all-to-all-done.5 = bf16[2,1024,192]{2,0,1:T(2,128)(2,1)S(1)} async-done(((bf16[2,1024,192]{2,0,1:T(2,128)(2,1)}), bf16[2,1024,192]{2,0,1:T(2,128)(2,1)S(1)}, u32[]{:S(2)}, u32[]{:S(2)}) %all-to-all-start.5) | async-done | bytes 786464 | tf_op jit(solution)/shard_map/all_to_all | solution.py:220
  357.2 9.0 copy.168
  371.0 6.9 convolution_bitcast_fusion
  377.9 11.5 %copy.145 = f32[8,4,384,192]{3,2,1,0:T(8,128)} copy(f32[8,4,384,192]{2,3,1,0:T(8,128)} %convolution_bitcast_fusion) | data formatting | bytes 18874368 | tf_op jit(solution)/shard_map/transpose | solution.py:106
  389.4 11.1 %concatenate.41 = f32[32,73728]{1,0:T(8,128)} reshape(f32[8,4,384,192]{3,2,1,0:T(8,128)} %copy.145) | data formatting | bytes 18874368 | tf_op jit(solution)/shard_map/concatenate | solution.py:304
  444.8 8.6 concatenate.37
  456.3 20.7 %dynamic-update-slice.3 = f32[32,243904]{1,0:T(8,128)} dynamic-update-slice(f32[32,243904]{1,0:T(8,128)} %dynamic-update-slice.2, f32[32,55296]{1,0:T(8,128)} %concatenate.37, s32[]{} %constant.108, s32[]{} %constant.111) | dynamic-update-slice | bytes 14155780
  476.9 8.9 dynamic-update-slice.4
  487.4 28.8 %dynamic-update-slice.6 = f32[32,243904]{1,0:T(8,128)} dynamic-update-slice(f32[32,243904]{1,0:T(8,128)} %dynamic-update-slice.5, f32[32,73728]{1,0:T(8,128)} %bitcast.326, s32[]{} %constant.108, s32[]{} %constant.114) | dynamic-update-slice | bytes 18874372
  516.1 28.6 %dynamic-update-slice.7 = f32[32,243904]{1,0:T(8,128)} dynamic-update-slice(f32[32,243904]{1,0:T(8,128)} %dynamic-update-slice.6, f32[32,73728]{1,0:T(8,128)} %concatenate.41, s32[]{} %constant.108, s32[]{} %constant.115) | dynamic-update-slice | bytes 18874372 | tf_op jit(solution)/shard_map/concatenate | solution.py:304
  544.8 469.4 %all-reduce.7.cloned.1.call-done = f32[32,243904]{1,0:T(8,128)} async-done(((f32[32,243904]{1,0:T(8,128)}), f32[32,243904]{1,0:T(8,128)}) %all-reduce.7.cloned.1.call-update) | async-done | bytes 31219728
  (335 shorter events, 255.8 us)
Async XLA Ops:
  7.2 153.2 %copy-start = (bf16[768,768]{1,0:T(8,128)(2,1)S(1)}, bf16[768,768]{1,0:T(8,128)(2,1)}, u32[]{:S(2)}) copy-start(bf16[768,768]{1,0:T(8,128)(2,1)} %param.23) | copy-start | bytes 3538948
  10.6 6.6 copy-start.9
  22.9 8.1 copy-start.62
  24.7 26.4 %all-to-all-start = ((bf16[2,256,768]{1,0,2:T(2,128)(2,1)}), bf16[2,256,768]{1,0,2:T(2,128)(2,1)S(1)}, u32[]{:S(2)}, u32[]{:S(2)}) async-start(bf16[2,256,768]{1,0,2:T(2,128)(2,1)} %copy.112), calls=%async_computation | async-start | bytes 1572864 | tf_op jit(solution)/shard_map/all_to_all | solution.py:176
  51.1 23.1 %all-to-all-start.1 = ((bf16[2,256,768]{1,0,2:T(2,128)(2,1)}), bf16[2,256,768]{1,0,2:T(2,128)(2,1)S(1)}, u32[]{:S(2)}, u32[]{:S(2)}) async-start(bf16[2,256,768]{1,0,2:T(2,128)(2,1)} %copy.115), calls=%async_computation.1 | async-start | bytes 1572864 | tf_op jit(solution)/shard_map/all_to_all | solution.py:174
  74.2 24.4 %all-to-all-start.2 = ((bf16[2,256,768]{1,0,2:T(2,128)(2,1)}), bf16[2,256,768]{1,0,2:T(2,128)(2,1)}, u32[]{:S(2)}, u32[]{:S(2)}) async-start(bf16[2,256,768]{1,0,2:T(2,128)(2,1)} %copy.117), calls=%async_computation.2 | async-start | bytes 1572864 | tf_op jit(solution)/shard_map/all_to_all | solution.py:175
  122.0 8.1 copy-start.61
  125.6 29.7 %all-to-all-start.3 = ((bf16[2,1024,192]{2,0,1:T(2,128)(2,1)}), bf16[2,1024,192]{2,0,1:T(2,128)(2,1)}, u32[]{:S(2)}, u32[]{:S(2)}) async-start(bf16[2,1024,192]{2,0,1:T(2,128)(2,1)} %copy.119), calls=%async_computation.3 | async-start | bytes 2097152 | tf_op jit(solution)/shard_map/all_to_all | solution.py:179
  160.4 16.4 %slice-start.2 = ((s8[4718592]{0:T(1024)(128)(4,1)}), s8[4194304]{0:T(1024)(128)(4,1)S(1)}, s32[]{:S(2)}) async-start(s8[4718592]{0:T(1024)(128)(4,1)} %bitcast.371), calls=%async_computation.11 | async-start | bytes 8388608
  163.6 21.6 %slice-start.4 = ((s8[4718592]{0:T(1024)(128)(4,1)}), s8[4194304]{0:T(1024)(128)(4,1)S(1)}, s32[]{:S(2)}) async-start(s8[4718592]{0:T(1024)(128)(4,1)} %bitcast.373), calls=%async_computation.13 | async-start | bytes 8388608
  164.0 12.8 %copy-start.31 = (bf16[2,256,768]{2,1,0:T(8,128)(2,1)}, bf16[2,256,768]{2,1,0:T(8,128)(2,1)S(1)}, u32[]{:S(2)}) copy-start(bf16[2,256,768]{2,1,0:T(8,128)(2,1)S(1)} %add_convert_fusion.2) | copy-start | bytes 2359300
  164.0 12.8 %slice-start.3 = ((s8[4718592]{0:T(1024)(128)(4,1)}), s8[524288]{0:T(1024)(128)(4,1)S(1)}, s32[]{:S(2)}) async-start(s8[4718592]{0:T(1024)(128)(4,1)} %bitcast.371), calls=%async_computation.12 | async-start | bytes 1048576
  164.0 21.2 %slice-start.5 = ((s8[4718592]{0:T(1024)(128)(4,1)}), s8[524288]{0:T(1024)(128)(4,1)S(1)}, s32[]{:S(2)}) async-start(s8[4718592]{0:T(1024)(128)(4,1)} %bitcast.373), calls=%async_computation.14 | async-start | bytes 1048576
  275.1 7.2 copy-start.23
  278.7 28.3 %all-to-all-start.7 = ((bf16[2,1024,192]{2,0,1:T(2,128)(2,1)}), bf16[2,1024,192]{2,0,1:T(2,128)(2,1)S(1)}, u32[]{:S(2)}, u32[]{:S(2)}) async-start(bf16[2,1024,192]{2,0,1:T(2,128)(2,1)} %copy.130), calls=%async_computation.7 | async-start | bytes 2097152 | tf_op jit(solution)/shard_map/all_to_all | solution.py:222
  282.3 33.0 %copy-start.8 = (bf16[2,4,256,192]{2,1,3,0:T(4,128)(2,1)S(1)}, bf16[2,4,256,192]{2,1,3,0:T(4,128)(2,1)}, u32[]{:S(2)}) copy-start(bf16[2,4,256,192]{2,1,3,0:T(4,128)(2,1)} %copy.160) | copy-start | bytes 2359300
  307.0 28.9 %all-to-all-start.5 = ((bf16[2,1024,192]{2,0,1:T(2,128)(2,1)}), bf16[2,1024,192]{2,0,1:T(2,128)(2,1)S(1)}, u32[]{:S(2)}, u32[]{:S(2)}) async-start(bf16[2,1024,192]{2,0,1:T(2,128)(2,1)} %copy.126), calls=%async_computation.5 | async-start | bytes 2097152 | tf_op jit(solution)/shard_map/all_to_all | solution.py:220
  335.9 8.1 copy-start.16
  335.9 66.2 %all-to-all-start.6 = ((bf16[2,1024,192]{2,0,1:T(2,128)(2,1)}), bf16[2,1024,192]{2,0,1:T(2,128)(2,1)}, u32[]{:S(2)}, u32[]{:S(2)}) async-start(bf16[2,1024,192]{2,0,1:T(2,128)(2,1)} %copy.128), calls=%async_computation.6 | async-start | bytes 2097152 | tf_op jit(solution)/shard_map/all_to_all | solution.py:221
  340.1 674.1 %all-reduce.7.cloned.1.call-start = ((), (), s32[]{:S(2)}) async-start(), calls=%async_computation.8 | async-start | bytes 62455808
  389.4 11.8 %copy-start.17 = (bf16[2,1024,192]{2,0,1:T(2,128)(2,1)S(1)}, bf16[2,1024,192]{2,0,1:T(2,128)(2,1)}, u32[]{:S(2)}) copy-start(bf16[2,1024,192]{2,0,1:T(2,128)(2,1)} %copy-done.16) | copy-start | bytes 2359300
  444.8 8.6 copy-start.6
  456.2 20.7 %copy-start.7 = (f32[32,18432]{1,0:T(8,128)S(1)}, f32[32,18432]{1,0:T(8,128)}, u32[]{:S(2)}) copy-start(f32[32,18432]{1,0:T(8,128)} %concatenate.38) | copy-start | bytes 7077892
  544.7 484.5 %copy-start.1 = (bf16[768,768]{1,0:T(8,128)(2,1)S(1)}, bf16[768,768]{1,0:T(8,128)(2,1)}, u32[]{:S(2)}) copy-start(bf16[768,768]{1,0:T(8,128)(2,1)} %param.23) | copy-start | bytes 3538948
  (66 other events, 191.1 us)
Sparse Core Ops, SparseCore 0:
  544.9 469.2 all-reduce.6
where the time goes:
time: 1050 us; the launch traced here: 1040 us
  waiting for transfers between devices  567 us (54%)
  local copies, waits for them, and re-layouts  259 us (25%)
  matrix products  108 us (10%)
  other arithmetic  34.6 us (3%)
  starting transfers between devices  30.4 us (3%)
  blocking collectives  22.1 us (2%)
  between operations  15.5 us (1%)
    unnamed x2, waiting for transfers between devices  469 us
    unnamed x139, local copies, waits for them, and re-layouts  85.9 us
    concatenate x6, local copies, waits for them, and re-layouts, on_device(): stacked = jnp.concatenate(block_list, axis=2)  58.1 us
    all_to_all x1, waiting for transfers between devices, on_device(): lax.all_to_all(d_value_heads, 'narrow', split_axis=1, concat_axis=2, tile...  22.7 us
    all_to_all x1, blocking collectives, on_device(): lax.all_to_all(d_attended, 'narrow', split_axis=2, concat_axis=1, tiled=T...  22.1 us
  transfers between devices with their start and end apart: 8, of which 7 were waited for; matrix products, arithmetic and copies ran while one was open for 9% of the time, Pallas kernels for 0%

commit v1 on v0

--- a/solution.py
+++ b/solution.py
@@ -6,6 +6,22 @@
 HEAD_DIM = 64
 HIGHEST = lax.Precision.HIGHEST
 norm_eps = 1e-05
+
+
+def exchange_in_pairs(x, axis, split, join):
+    ways, here = (lax.axis_size(axis), lax.axis_index(axis))
+    width = x.shape[split] // ways
+    dims = list(x.shape)
+    dims[split] = width
+    height = dims[join]
+    dims[join] = height * ways
+    full = jnp.zeros(dims, x.dtype)
+    for mask in range(ways):
+        part = lax.dynamic_slice_in_dim(x, (here ^ mask) * width, width, axis=split)
+        if mask:
+            part = lax.ppermute(part, axis, [(d, d ^ mask) for d in range(ways)])
+        full = lax.dynamic_update_slice_in_dim(full, part, (here ^ mask) * height, axis=join)
+    return full
 
 
 def norm_mod(hidden, gain, shift, scale):
@@ -172,7 +188,7 @@
     value_low = qkv[:, :, 2].astype(jnp.bfloat16).reshape(row_count, part_len, model_width)
     query_heads, key_heads, value_heads = (
         lax.all_to_all(query_low, "narrow", split_axis=2, concat_axis=1, tiled=True),
-        lax.all_to_all(key_low, "narrow", split_axis=2, concat_axis=1, tiled=True),
+        exchange_in_pairs(key_low, "narrow", 2, 1),
         lax.all_to_all(value_low, "narrow", split_axis=2, concat_axis=1, tiled=True),
     )
     attended_heads, log_totals = lax.map(attend, (query_heads, key_heads, value_heads))

time: 1050 us -> 1040 us (level)
    ppermute x0 -> x3, waiting for transfers between devices: none -> 25.9 us  [exchange_in_pairs(): part = lax.ppermute(part, axis, [(d, d ^ mask) for d in range(ways)])]
    all_to_all x1, waiting for transfers between devices: 16.7 us -> 0.01 us  [on_device(): lax.all_to_all(query_low, 'narrow', split_axis=2, concat_axis=1, tiled=True)]
    all_to_all x1 -> x0, waiting for transfers between devices: 13 us -> none  [on_device(): lax.all_to_all(key_low, 'narrow', split_axis=2, concat_axis=1, tiled=True)]
    unnamed x139 -> x141, local copies, waits for them, and re-layouts: 85.9 us -> 86.9 us
  transfers between devices with their start and end apart: 8 -> 10, of which waited for: 7 -> 7; matrix products, arithmetic and copies ran while one was open for 9% -> 9% of each run, Pallas kernels for 0% -> 0%
where the time goes in v1:
time: 1040 us; the launch traced here: 1030 us
  waiting for transfers between devices  563 us (54%)
  local copies, waits for them, and re-layouts  258 us (25%)
  matrix products  108 us (10%)
  other arithmetic  34.7 us (3%)
  starting transfers between devices  31.3 us (3%)
  blocking collectives  22.7 us (2%)
  between operations  15.6 us (2%)
    unnamed x2, waiting for transfers between devices  470 us
    unnamed x141, local copies, waits for them, and re-layouts  86.9 us
    concatenate x6, local copies, waits for them, and re-layouts, on_device(): stacked = jnp.concatenate(block_list, axis=2)  58.1 us
    ppermute x3, waiting for transfers between devices, exchange_in_pairs(): part = lax.ppermute(part, axis, [(d, d ^ mask) for d in range(ways)])  25.9 us
    all_to_all x1, blocking collectives, on_device(): lax.all_to_all(d_attended, 'narrow', split_axis=2, concat_axis=1, tiled=T...  22.7 us
    all_to_all x1, waiting for transfers between devices, on_device(): lax.all_to_all(d_value_heads, 'narrow', split_axis=1, concat_axis=2, tile...  22.5 us
  transfers between devices with their start and end apart: 10, of which 7 were waited for; matrix products, arithmetic and copies ran while one was open for 9% of the time, Pallas kernels for 0%

profile of v1, /device:TPU:0, one launch (start us, length us, event | category | flops | bytes accessed | tf_op | source)
XLA Modules:
  0.0 1032.9 jit_solution(11211936486058706057)
XLA Ops:
  24.7 6.3 all-to-all-start
  36.9 14.2 %all-to-all-done = bf16[2,256,768]{1,0,2:T(2,128)(2,1)S(1)} async-done(((bf16[2,256,768]{1,0,2:T(2,128)(2,1)}), bf16[2,256,768]{1,0,2:T(2,128)(2,1)S(1)}, u32[]{:S(2)}, u32[]{:S(2)}) %all-to-all-start) | async-done | bytes 786464 | tf_op jit(solution)/shard_map/all_to_all | solution.py:192
  62.4 11.8 %collective-permute-done = bf16[2,256,192]{1,2,0:T(8,128)(2,1)} collective-permute-done((bf16[2,256,192]{1,2,0:T(8,128)(2,1)}, bf16[2,256,192]{1,2,0:T(8,128)(2,1)}, u32[]{:S(2)}, u32[]{:S(2)}) %collective-permute-start) | collective-permute-done | bytes 196640 | tf_op jit(solution)/shard_map/ppermute | solution.py:22
  75.1 14.1 %collective-permute-done.1 = bf16[2,256,192]{1,2,0:T(8,128)(2,1)} collective-permute-done((bf16[2,256,192]{1,2,0:T(8,128)(2,1)}, bf16[2,256,192]{1,2,0:T(8,128)(2,1)}, u32[]{:S(2)}, u32[]{:S(2)}) %collective-permute-start.1) | collective-permute-done | bytes 196640 | tf_op jit(solution)/shard_map/ppermute | solution.py:22
  100.8 17.3 %while.26 = (s32[]{:T(128)}, bf16[2,1024,192]{1,2,0:T(8,128)(2,1)}, f32[2,3,1024,1]{2,1,3,0:T(4,128)}, bf16[2,1024,192]{1,2,0:T(8,128)(2,1)S(1)}, bf16[2,1024,19...) while((s32[]{:T(128)}, bf16[2,1024,192]{1,2,0:T(8,128)(2,1)}, ...), condition=%wide.region_5.6_spmd, body=%wide.region_2.5_spmd.sunk | while | flops 833811456 | bytes 48861340 | solution.py:194
  126.2 7.9 fusion.85
  134.0 16.9 %all-to-all-done.2 = bf16[2,1024,192]{2,0,1:T(2,128)(2,1)} async-done(((bf16[2,1024,192]{2,0,1:T(2,128)(2,1)}), bf16[2,1024,192]{2,0,1:T(2,128)(2,1)}, u32[]{:S(2)}, u32[]{:S(2)}) %all-to-all-start.2) | async-done | bytes 786464 | tf_op jit(solution)/shard_map/all_to_all | solution.py:195
  159.7 12.8 %fusion.27 = (bf16[3072,512]{0,1:T(8,128)(2,1)}, bf16[3072,512]{0,1:T(8,128)(2,1)}, f32[512,3072]{1,0:T(8,128)}) fusion(f32[512,3072]{1,0:T(8,128)S(1)} %copy-done.65, bf16[512,768]{1,0:T(8,128)(2,1)S(1)} %bitcast.351, bf16[768,3072]{1,0:T(8,128)(2,1)} %param.25), kind=kOutput, calls=%fused_computation.51 | convolution fusion | flops 2450522112 | bytes 24379392 | tf_op jit(solution)/shard_map/dot_general | solution.py:207
  172.5 8.4 fusion.34
  180.9 6.3 fusion.33
  198.0 22.7 %all_to_all.96 = bf16[2,256,768]{1,0,2:T(2,128)(2,1)S(1)} all-to-all(bf16[2,256,768]{1,0,2:T(2,128)(2,1)S(1)} %copy.118), channel_id=1, replica_groups=mesh['wide'=8,'narrow'=4] {'narrow'}, dimensions={2} | all-to-all | bytes 1572864 | tf_op jit(solution)/shard_map/all_to_all | solution.py:231
  224.8 46.7 %while.27 = (s32[]{:T(128)}, bf16[2,1024,192]{1,2,0:T(8,128)(2,1)}, bf16[2,1024,192]{1,2,0:T(8,128)(2,1)}, bf16[2,1024,192]{1,2,0:T(8,128)(2,1)}, bf16[2,1024,19...) while((s32[]{:T(128)}, bf16[2,1024,192]{1,2,0:T(8,128)(2,1)}, ...), condition=%wide.region_12.13_spmd, body=%wide.region_10.12_spmd.sunk | while | flops 2051994624 | bytes 144789888 | solution.py:232
  280.7 22.5 %all-to-all-done.6 = bf16[2,1024,192]{2,0,1:T(2,128)(2,1)S(1)} async-done(((bf16[2,1024,192]{2,0,1:T(2,128)(2,1)}), bf16[2,1024,192]{2,0,1:T(2,128)(2,1)S(1)}, u32[]{:S(2)}, u32[]{:S(2)}) %all-to-all-start.6) | async-done | bytes 786464 | tf_op jit(solution)/shard_map/all_to_all | solution.py:238
  318.4 13.7 %all-to-all-done.4 = bf16[2,1024,192]{2,0,1:T(2,128)(2,1)S(1)} async-done(((bf16[2,1024,192]{2,0,1:T(2,128)(2,1)}), bf16[2,1024,192]{2,0,1:T(2,128)(2,1)S(1)}, u32[]{:S(2)}, u32[]{:S(2)}) %all-to-all-start.4) | async-done | bytes 786464 | tf_op jit(solution)/shard_map/all_to_all | solution.py:236
  353.5 9.0 copy.163
  367.3 6.9 convolution_bitcast_fusion
  374.1 11.5 %copy.140 = f32[8,4,384,192]{3,2,1,0:T(8,128)} copy(f32[8,4,384,192]{2,3,1,0:T(8,128)} %convolution_bitcast_fusion) | data formatting | bytes 18874368 | tf_op jit(solution)/shard_map/transpose | solution.py:122
  385.6 11.1 %concatenate.41 = f32[32,73728]{1,0:T(8,128)} reshape(f32[8,4,384,192]{3,2,1,0:T(8,128)} %copy.140) | data formatting | bytes 18874368 | tf_op jit(solution)/shard_map/concatenate | solution.py:320
  441.0 8.6 concatenate.37
  452.5 20.7 %dynamic-update-slice.3 = f32[32,243904]{1,0:T(8,128)} dynamic-update-slice(f32[32,243904]{1,0:T(8,128)} %dynamic-update-slice.2, f32[32,55296]{1,0:T(8,128)} %concatenate.37, s32[]{} %constant.126, s32[]{} %constant.129) | dynamic-update-slice | bytes 14155780
  473.2 8.9 dynamic-update-slice.4
  483.6 28.8 %dynamic-update-slice.6 = f32[32,243904]{1,0:T(8,128)} dynamic-update-slice(f32[32,243904]{1,0:T(8,128)} %dynamic-update-slice.5, f32[32,73728]{1,0:T(8,128)} %bitcast.321, s32[]{} %constant.126, s32[]{} %constant.132) | dynamic-update-slice | bytes 18874372
  512.4 28.6 %dynamic-update-slice.7 = f32[32,243904]{1,0:T(8,128)} dynamic-update-slice(f32[32,243904]{1,0:T(8,128)} %dynamic-update-slice.6, f32[32,73728]{1,0:T(8,128)} %concatenate.41, s32[]{} %constant.126, s32[]{} %constant.133) | dynamic-update-slice | bytes 18874372 | tf_op jit(solution)/shard_map/concatenate | solution.py:320
  541.0 469.5 %all-reduce.7.cloned.1.call-done = f32[32,243904]{1,0:T(8,128)} async-done(((f32[32,243904]{1,0:T(8,128)}), f32[32,243904]{1,0:T(8,128)}) %all-reduce.7.cloned.1.call-update) | async-done | bytes 31219728
  (343 shorter events, 255.8 us)
Async XLA Ops:
  7.2 148.8 %copy-start = (bf16[768,768]{1,0:T(8,128)(2,1)S(1)}, bf16[768,768]{1,0:T(8,128)(2,1)}, u32[]{:S(2)}) copy-start(bf16[768,768]{1,0:T(8,128)(2,1)} %param.23) | copy-start | bytes 3538948
  22.9 8.1 copy-start.63
  24.7 26.4 %all-to-all-start = ((bf16[2,256,768]{1,0,2:T(2,128)(2,1)}), bf16[2,256,768]{1,0,2:T(2,128)(2,1)S(1)}, u32[]{:S(2)}, u32[]{:S(2)}) async-start(bf16[2,256,768]{1,0,2:T(2,128)(2,1)} %copy.109), calls=%async_computation | async-start | bytes 1572864 | tf_op jit(solution)/shard_map/all_to_all | solution.py:192
  51.1 44.3 %all-to-all-start.1 = ((bf16[2,256,768]{1,0,2:T(2,128)(2,1)}), bf16[2,256,768]{1,0,2:T(2,128)(2,1)}, u32[]{:S(2)}, u32[]{:S(2)}) async-start(bf16[2,256,768]{1,0,2:T(2,128)(2,1)} %copy.112), calls=%async_computation.1 | async-start | bytes 1572864 | tf_op jit(solution)/shard_map/all_to_all | solution.py:190
  58.0 16.2 %collective-permute-start = (bf16[2,256,192]{1,2,0:T(8,128)(2,1)}, bf16[2,256,192]{1,2,0:T(8,128)(2,1)}, u32[]{:S(2)}, u32[]{:S(2)}) collective-permute-start(bf16[2,256,192]{1,2,0:T(8,128)(2,1)} %get-tuple-element.200), channel_id=1, source_target_pairs={{0,1},{1,0},{2,3},{3,2},{4,5},{5,4},{6,7},{7,6},{8,9},{9,8},{10,11... | collective-permute-start | bytes 589832 | tf_op jit(solution)/shard_map/ppermute | solution.py:22
  60.0 29.2 %collective-permute-start.1 = (bf16[2,256,192]{1,2,0:T(8,128)(2,1)}, bf16[2,256,192]{1,2,0:T(8,128)(2,1)}, u32[]{:S(2)}, u32[]{:S(2)}) collective-permute-start(bf16[2,256,192]{1,2,0:T(8,128)(2,1)} %get-tuple-element.199), channel_id=1, source_target_pairs={{0,2},{1,3},{2,0},{3,1},{4,6},{5,7},{6,4},{7,5},{8,10},{9,11},{10,... | collective-permute-start | bytes 589832 | tf_op jit(solution)/shard_map/ppermute | solution.py:22
  62.3 27.8 %collective-permute-start.2 = (bf16[2,256,192]{1,2,0:T(8,128)(2,1)}, bf16[2,256,192]{1,2,0:T(8,128)(2,1)}, u32[]{:S(2)}, u32[]{:S(2)}) collective-permute-start(bf16[2,256,192]{1,2,0:T(8,128)(2,1)} %get-tuple-element.198), channel_id=1, source_target_pairs={{0,3},{1,2},{2,1},{3,0},{4,7},{5,6},{6,5},{7,4},{8,11},{9,10},{10,... | collective-permute-start | bytes 589832 | tf_op jit(solution)/shard_map/ppermute | solution.py:22
  118.1 8.1 copy-start.62
  121.7 29.3 %all-to-all-start.2 = ((bf16[2,1024,192]{2,0,1:T(2,128)(2,1)}), bf16[2,1024,192]{2,0,1:T(2,128)(2,1)}, u32[]{:S(2)}, u32[]{:S(2)}) async-start(bf16[2,1024,192]{2,0,1:T(2,128)(2,1)} %copy.114), calls=%async_computation.2 | async-start | bytes 2097152 | tf_op jit(solution)/shard_map/all_to_all | solution.py:195
  156.0 16.4 %slice-start.2 = ((s8[4718592]{0:T(1024)(128)(4,1)}), s8[4194304]{0:T(1024)(128)(4,1)S(1)}, s32[]{:S(2)}) async-start(s8[4718592]{0:T(1024)(128)(4,1)} %bitcast.365), calls=%async_computation.10 | async-start | bytes 8388608
  159.2 21.7 %slice-start.4 = ((s8[4718592]{0:T(1024)(128)(4,1)}), s8[4194304]{0:T(1024)(128)(4,1)S(1)}, s32[]{:S(2)}) async-start(s8[4718592]{0:T(1024)(128)(4,1)} %bitcast.367), calls=%async_computation.12 | async-start | bytes 8388608
  159.6 12.8 %copy-start.32 = (bf16[2,256,768]{2,1,0:T(8,128)(2,1)}, bf16[2,256,768]{2,1,0:T(8,128)(2,1)S(1)}, u32[]{:S(2)}) copy-start(bf16[2,256,768]{2,1,0:T(8,128)(2,1)S(1)} %add_convert_fusion.2) | copy-start | bytes 2359300
  159.6 12.8 %slice-start.3 = ((s8[4718592]{0:T(1024)(128)(4,1)}), s8[524288]{0:T(1024)(128)(4,1)S(1)}, s32[]{:S(2)}) async-start(s8[4718592]{0:T(1024)(128)(4,1)} %bitcast.365), calls=%async_computation.11 | async-start | bytes 1048576
  159.6 21.2 %slice-start.5 = ((s8[4718592]{0:T(1024)(128)(4,1)}), s8[524288]{0:T(1024)(128)(4,1)S(1)}, s32[]{:S(2)}) async-start(s8[4718592]{0:T(1024)(128)(4,1)} %bitcast.367), calls=%async_computation.13 | async-start | bytes 1048576
  275.2 28.1 %all-to-all-start.6 = ((bf16[2,1024,192]{2,0,1:T(2,128)(2,1)}), bf16[2,1024,192]{2,0,1:T(2,128)(2,1)S(1)}, u32[]{:S(2)}, u32[]{:S(2)}) async-start(bf16[2,1024,192]{2,0,1:T(2,128)(2,1)} %copy.125), calls=%async_computation.6 | async-start | bytes 2097152 | tf_op jit(solution)/shard_map/all_to_all | solution.py:238
  278.7 32.8 %copy-start.9 = (bf16[2,4,256,192]{2,1,3,0:T(4,128)(2,1)S(1)}, bf16[2,4,256,192]{2,1,3,0:T(4,128)(2,1)}, u32[]{:S(2)}) copy-start(bf16[2,4,256,192]{2,1,3,0:T(4,128)(2,1)} %copy.155) | copy-start | bytes 2359300
  303.3 28.9 %all-to-all-start.4 = ((bf16[2,1024,192]{2,0,1:T(2,128)(2,1)}), bf16[2,1024,192]{2,0,1:T(2,128)(2,1)S(1)}, u32[]{:S(2)}, u32[]{:S(2)}) async-start(bf16[2,1024,192]{2,0,1:T(2,128)(2,1)} %copy.121), calls=%async_computation.4 | async-start | bytes 2097152 | tf_op jit(solution)/shard_map/all_to_all | solution.py:236
  332.1 8.1 copy-start.17
  332.1 66.1 %all-to-all-start.5 = ((bf16[2,1024,192]{2,0,1:T(2,128)(2,1)}), bf16[2,1024,192]{2,0,1:T(2,128)(2,1)}, u32[]{:S(2)}, u32[]{:S(2)}) async-start(bf16[2,1024,192]{2,0,1:T(2,128)(2,1)} %copy.123), calls=%async_computation.5 | async-start | bytes 2097152 | tf_op jit(solution)/shard_map/all_to_all | solution.py:237
  336.4 674.1 %all-reduce.7.cloned.1.call-start = ((), (), s32[]{:S(2)}) async-start(), calls=%async_computation.7 | async-start | bytes 62455808
  385.6 11.8 %copy-start.18 = (bf16[2,1024,192]{2,0,1:T(2,128)(2,1)S(1)}, bf16[2,1024,192]{2,0,1:T(2,128)(2,1)}, u32[]{:S(2)}) copy-start(bf16[2,1024,192]{2,0,1:T(2,128)(2,1)} %copy-done.17) | copy-start | bytes 2359300
  441.0 8.6 copy-start.7
  452.5 20.7 %copy-start.8 = (f32[32,18432]{1,0:T(8,128)S(1)}, f32[32,18432]{1,0:T(8,128)}, u32[]{:S(2)}) copy-start(f32[32,18432]{1,0:T(8,128)} %concatenate.38) | copy-start | bytes 7077892
  541.0 484.5 %copy-start.1 = (bf16[768,768]{1,0:T(8,128)(2,1)S(1)}, bf16[768,768]{1,0:T(8,128)(2,1)}, u32[]{:S(2)}) copy-start(bf16[768,768]{1,0:T(8,128)(2,1)} %param.23) | copy-start | bytes 3538948
  (69 other events, 205.6 us)
Sparse Core Ops, SparseCore 0:
  541.1 469.3 all-reduce.6
